TPU v7x, 128 devices: a whole 4x4x4 slice. The times are simulated.
128 devices in a mesh: row: 8 (over z_hi, y), col: 16 (over x, z_lo, core).
Axes of the slice: x: 4, y: 4, z: 4 (z_hi: 2, z_lo: 2; z = z_hi * 2 + z_lo), core: 2. Of those that a mesh axis runs over, the one named last changes fastest.
Arguments:
- sim: bfloat16 [16384, 16384], P('row', 'col'), may hold values from -6 to 6
- diag_blocks: bfloat16 [2048, 16384], P(None, 'col'), may hold values from -0.125 to 0.125
- match_perm: int32 [8, 2048], replicated, may hold values from 0 to 2047, each once within a row
- match_scale: float32 [8, 2048], replicated, may hold values from 0.3 to 1.5
- features: bfloat16 [16384, 256], P('col'), may hold values from -0.046875 to 0.046875
Outputs:
- new_sim: bfloat16 [16384, 16384], P('row', 'col')
- aggregated: float32 [16384, 256], P(('row', 'col'))
Inputs may be any that keep to these rules, and one draw needn't show every extreme that they name: Each row of match_perm lists every number of 0 to 2047 once.
All inputs are finite; a program needn't handle non-finite values.
Results may differ from a plain program's by a relative error of at most 0.0058.
Values may be sent and summed in bfloat16 or wider, within the bound.
A program may use at most 128 MiB of HBM per device.

v0:
```python
import jax
import jax.numpy as jnp
from jax import lax
from jax.sharding import PartitionSpec as P

decay_factor = 0.8


def partner_2(value, axis, bit):
    mask = 2**bit
    pairs = [(source, source ^ mask) for source in range(lax.axis_size(axis))]
    return lax.ppermute(value, axis, pairs)


def shifted(value, axis, steps):
    count = lax.axis_size(axis)
    pairs = [(source, (source + steps) % count) for source in range(count)]
    return lax.ppermute(value, axis, pairs)


def rows_for(lines, size):
    spare = -lines.shape[0] % size
    if not spare:
        return lines
    return jnp.concatenate([lines, jnp.zeros((spare, *lines.shape[1:]), lines.dtype)])


def broadcast_by_parts(x, axis, root):
    lines = jnp.where(lax.axis_index(axis) == root, x, jnp.zeros_like(x)).reshape(
        -1, *x.shape[1:][-1:]
    )
    padded = rows_for(lines, lax.axis_size(axis))
    own = lax.psum_scatter(padded, axis, scatter_dimension=0, tiled=True)
    return lax.all_gather(own, axis, axis=0, tiled=True)[: len(lines)].reshape(x.shape)


def split_up(x, dim, size):
    dims = x.shape
    parts = x.reshape(*dims[:dim], size, dims[dim] // size, *dims[dim + 1 :])
    return jnp.moveaxis(parts, dim, 0)


def sum_at_owner(x, axis, dim):
    size = lax.axis_size(axis)
    parts = lax.all_to_all(split_up(x, dim, size), axis, 0, 0, tiled=True)
    return jnp.sum(parts, axis=0)


def on_device(sim, diag_blocks, match_perm, match_scale, features):
    row_count = lax.axis_size("row")
    col_count = lax.axis_size("col")
    blocks_here = col_count // 2 // row_count
    row_id = lax.axis_index("row")
    col_id = lax.axis_index("col")
    block_id = col_id // 2
    side = col_id % 2
    half_width = sim.shape[1]
    tile_rows = sim.shape[0]
    partner = partner_2(sim, "col", 0)
    first_half = jnp.where(side == 0, sim, partner)
    second_half = jnp.where(side == 0, partner, sim)
    whole_block = jnp.concatenate([first_half, second_half], axis=1)
    perm_block = lax.dynamic_index_in_dim(match_perm, block_id, 0, keepdims=False)
    scale_block = lax.dynamic_index_in_dim(match_scale, block_id, 0, keepdims=False)
    own_perm = lax.dynamic_slice_in_dim(perm_block, side * half_width, half_width, 0)
    own_scale = lax.dynamic_slice_in_dim(scale_block, side * half_width, half_width, 0)
    moved_cols = (jnp.take(whole_block, own_perm, axis=1) * own_scale[None, :]).astype(jnp.bfloat16)
    arrived_cols = shifted(moved_cols, "col", col_count // 2)
    mixed = (
        jnp.dot(whole_block, diag_blocks, preferred_element_type=jnp.float32) + arrived_cols
    ).astype(jnp.bfloat16)
    position = 0
    source = row_id * blocks_here + position
    perm_rows = lax.dynamic_index_in_dim(match_perm, source, 0, keepdims=False)
    scale_rows = lax.dynamic_index_in_dim(match_scale, source, 0, keepdims=False)
    sent_rows = (jnp.take(mixed, perm_rows, axis=0) * scale_rows[:, None]).astype(jnp.bfloat16)
    arrived_rows = shifted(sent_rows, "row", row_count // 2)
    position = 0
    target = row_id * blocks_here + position
    halves = []
    for part in range(2):
        left_half = broadcast_by_parts(diag_blocks, "col", 2 * target + part)
        halves.append(
            lax.dot_general(
                left_half, mixed, (((0,), (0,)), ((), ())), preferred_element_type=jnp.float32
            )
        )
    product = jnp.concatenate(halves, axis=0)
    results = decay_factor * (product + arrived_rows)
    global_rows = row_id * tile_rows + lax.broadcasted_iota(jnp.int32, results.shape, 0)
    global_cols = col_id * half_width + lax.broadcasted_iota(jnp.int32, results.shape, 1)
    new_sim = jnp.where(global_rows == global_cols, 1.0, results).astype(jnp.bfloat16)
    partial_value = jnp.dot(new_sim, features, preferred_element_type=jnp.float32)
    aggregated = sum_at_owner(partial_value, "col", 0)
    return (new_sim, aggregated)


def solution(mesh):
    placed = (P("row", "col"), P(None, "col"), P(), P(), P("col", None))
    return jax.shard_map(
        on_device,
        mesh=mesh,
        in_specs=placed,
        out_specs=(P("row", "col"), P(("row", "col"), None)),
        check_vma=False,
    )
```

profile of v0, /device:TPU:1, one launch (start us, length us, event | category | flops | bytes accessed | tf_op | source)
XLA Modules:
  0.0 425.5 jit_solution(9150470076904124508)
XLA Ops:
  7.2 0.0 reduce-scatter.3.cloned.1.call-start
  7.2 6.1 %broadcast_select_fusion.3 = (bf16[2048,1024]{1,0:T(8,128)(2,1)}, bf16[2048,1024]{1,0:T(8,128)(2,1)}) fusion(bf16[2048,1024]{1,0:T(8,128)(2,1)} %param.6, pred[]{:T(512)S(6)} %eq.16, pred[]{:T(512)S(6)} %eq.18), kind=kLoop, calls=%fused_computation.14 | loop fusion | flops 4194304 | bytes 12582914 | tf_op jit(solution)/shard_map/jit(_where)/select_n | solution.py:29
  13.3 0.0 reduce-scatter.5.cloned.1.call-start
  13.4 0.7 reduce-scatter.5.cloned.1.call-update
  14.1 0.0 all-gather.3.cloned.1.call-start
  14.1 6.5 %copy.12 = bf16[2048,1024]{0,1:T(8,128)(2,1)} copy(bf16[2048,1024]{1,0:T(8,128)(2,1)} %param.5) | data formatting | bytes 8388608 | tf_op args[0]
  20.7 1.4 collective-permute-start
  22.1 60.6 %reduce-scatter.3.cloned.1.call-done = bf16[128,1024]{1,0:T(8,128)(2,1)} async-done(((bf16[2048,1024]{1,0:T(8,128)(2,1)}), bf16[128,1024]{1,0:T(8,128)(2,1)}) %reduce-scatter.3.cloned.1.call-update) | async-done | bytes 262160 | tf_op jit(solution)/shard_map/reduce_scatter | solution.py:33
  82.8 0.8 dynamic_slice.23
  83.6 0.8 compare_select_fusion.1
  84.5 5.9 %broadcast_select_fusion.2 = (bf16[2048,1024]{0,1:T(8,128)(2,1)}, bf16[2048,1024]{0,1:T(8,128)(2,1)}) fusion(bf16[2048,1024]{0,1:T(8,128)(2,1)} %copy.12, bf16[2048,1024]{0,1:T(8,128)(2,1)} %collective-permute-done, pred[]{:T(512)S(6)} %eq.17), kind=kLoop, calls=%fused_computation.13 | loop fusion | flops 4194304 | bytes 16777216 | tf_op jit(solution)/shard_map/jit(_where)/select_n | solution.py:60
  90.4 8.4 %pad_maximum_fusion = bf16[2048,2048]{0,1:T(8,128)(2,1)} fusion(bf16[2048,1024]{0,1:T(8,128)(2,1)} %get-tuple-element.7, bf16[2048,1024]{0,1:T(8,128)(2,1)} %get-tuple-element.6), kind=kLoop, calls=%fused_computation.2 | loop fusion | flops 16777216 | bytes 16777216 | tf_op jit(solution)/shard_map/concatenate | solution.py:62
  98.7 13.4 %gather_fusion = bf16[1024,2048]{1,0:T(8,128)(2,1)} fusion(bf16[2048,2048]{0,1:T(8,128)(2,1)} %pad_maximum_fusion, s32[1024]{0:T(1024)S(1)} %broadcast_clamp_fusion.1), kind=kCustom, calls=%fused_computation | custom fusion | bytes 8392704 | tf_op jit(solution)/shard_map/jit(_take)/gather | solution.py:67
  112.1 6.4 %copy.14 = bf16[1024,2048]{0,1:T(8,128)(2,1)} copy(bf16[1024,2048]{1,0:T(8,128)(2,1)} %gather_fusion) | data formatting | bytes 8388608 | tf_op jit(solution)/shard_map/jit(_take)/gather | solution.py:67
  118.5 5.4 %fusion.3 = bf16[2048,1024]{1,0:T(8,128)(2,1)} fusion(f32[1024]{0:T(1024)S(1)} %bitcast.24, bf16[1024,2048]{0,1:T(8,128)(2,1)} %copy.14, pred[1024]{0:T(1024)(128)(4,1)S(1)} %compare_and_fusion.1), kind=kLoop, calls=%fused_computation.10 | loop fusion | flops 8388608 | bytes 8393728 | tf_op jit(solution)/shard_map/convert_element_type | solution.py:67
  123.9 104.8 %reduce-scatter.5.cloned.1.call-done = bf16[128,1024]{1,0:T(8,128)(2,1)} async-done(((bf16[2048,1024]{1,0:T(8,128)(2,1)}), bf16[128,1024]{1,0:T(8,128)(2,1)}) %reduce-scatter.5.cloned.1.call-update) | async-done | bytes 262160 | tf_op jit(solution)/shard_map/reduce_scatter | solution.py:33
  228.8 0.9 constant_dynamic-slice_fusion
  229.6 0.9 compare_select_fusion
  230.5 14.6 %add_convert_fusion = bf16[2048,1024]{1,0:T(8,128)(2,1)} fusion(bf16[2048,1024]{1,0:T(8,128)(2,1)} %collective-permute-done.1, bf16[2048,1024]{1,0:T(8,128)(2,1)} %param.6, bf16[2048,1024]{0,1:T(8,128)(2,1)} %get-tuple-element.7, bf16[2048,1024]{0,1:T(8,128)(2,1)} %get-tuple-element.6), kind=kOutput, calls=%fused_computation.9 | convolution fusion | flops 8613003264 | bytes 20971520 | tf_op jit(solution)/shard_map/dot_general | solution.py:70
  245.2 13.7 %gather_fusion.1 = bf16[2048,1024]{1,0:T(8,128)(2,1)} fusion(bf16[2048,1024]{1,0:T(8,128)(2,1)} %add_convert_fusion, s32[2048]{0:T(1024)S(1)} %broadcast_clamp_fusion), kind=kCustom, calls=%fused_computation.1 | custom fusion | bytes 8396800 | tf_op jit(solution)/shard_map/jit(_take)/gather | solution.py:76
  258.8 4.2 multiply_convert_fusion.1
  263.0 4.9 %collective-permute-start.2 = (bf16[2048,1024]{1,0:T(8,128)(2,1)}, bf16[2048,1024]{1,0:T(8,128)(2,1)}, u32[]{:S(2)}, u32[]{:S(2)}) collective-permute-start(bf16[2048,1024]{1,0:T(8,128)(2,1)} %multiply_convert_fusion.1), channel_id=1, source_target_pairs={{0,64},{16,80},{32,96},{48,112},{64,0},{80,16},{96,32},{112,48},{1... | collective-permute-start | bytes 12582920 | tf_op jit(solution)/shard_map/ppermute | solution.py:18
  267.9 10.5 %all-gather.3.cloned.1.call-done = bf16[2048,1024]{1,0:T(8,128)(2,1)} async-done(((bf16[128,1024]{1,0:T(8,128)(2,1)}), bf16[2048,1024]{1,0:T(8,128)(2,1)}) %all-gather.3.cloned.1.call-update) | async-done | bytes 4194320 | tf_op jit(solution)/shard_map/all_gather | solution.py:34
  278.4 10.0 %fusion.4 = f32[1024,1024]{1,0:T(8,128)} fusion(bf16[2048,1024]{1,0:T(8,128)(2,1)} %all-gather.3.cloned.1.call-done, bf16[2048,1024]{1,0:T(8,128)(2,1)} %add_convert_fusion), kind=kOutput, calls=%fused_computation.27 | convolution fusion | flops 4294967296 | bytes 12582912 | tf_op jit(solution)/shard_map/dot_general | solution.py:84
  288.4 43.2 %all-gather.5.cloned.1.call-done = bf16[2048,1024]{1,0:T(8,128)(2,1)} async-done(((bf16[128,1024]{1,0:T(8,128)(2,1)}), bf16[2048,1024]{1,0:T(8,128)(2,1)}) %all-gather.5.cloned.1.call-update) | async-done | bytes 4194320 | tf_op jit(solution)/shard_map/all_gather | solution.py:34
  331.6 7.7 %fusion.5 = f32[1024,1024]{1,0:T(8,128)S(1)} fusion(bf16[2048,1024]{1,0:T(8,128)(2,1)} %all-gather.5.cloned.1.call-done, bf16[2048,1024]{1,0:T(8,128)(2,1)} %add_convert_fusion), kind=kOutput, calls=%fused_computation.28 | convolution fusion | flops 4294967296 | bytes 12582912 | tf_op jit(solution)/shard_map/dot_general | solution.py:84
  339.4 42.7 %collective-permute-done.2 = bf16[2048,1024]{1,0:T(8,128)(2,1)} collective-permute-done((bf16[2048,1024]{1,0:T(8,128)(2,1)}, bf16[2048,1024]{1,0:T(8,128)(2,1)}, u32[]{:S(2)}, u32[]{:S(2)}) %collective-permute-start.2) | collective-permute-done | bytes 4194336 | tf_op jit(solution)/shard_map/ppermute | solution.py:18
  382.1 4.1 fusion.2
  386.2 1.3 fusion.6
  387.5 0.7 copy-done.1
  388.2 30.0 %all_to_all.5 = f32[16,128,256]{2,1,0:T(8,128)S(1)} all-to-all(f32[16,128,256]{2,1,0:T(8,128)S(1)} %bitcast.20), channel_id=1, replica_groups=mesh['row'=8,'col'=16] {'col'}, dimensions={0} | all-to-all | bytes 4194304 | tf_op jit(solution)/shard_map/all_to_all | solution.py:45
  418.2 0.8 reduce_sum.9
  (18 shorter events, 0.1 us)
Async XLA Ops:
  7.2 379.0 %copy-start = (bf16[1024,256]{1,0:T(8,128)(2,1)S(1)}, bf16[1024,256]{1,0:T(8,128)(2,1)}, u32[]{:S(2)}) copy-start(bf16[1024,256]{1,0:T(8,128)(2,1)} %param.9) | copy-start | bytes 1572868
  7.2 75.5 %reduce-scatter.3.cloned.1.call-start = ((), (), s32[]{:S(2)}) async-start(), calls=%async_computation.3 | async-start | bytes 4456448 | tf_op jit(solution)/shard_map/reduce_scatter | solution.py:33
  13.3 215.4 %reduce-scatter.5.cloned.1.call-start = ((), (), s32[]{:S(2)}) async-start(), calls=%async_computation.5 | async-start | bytes 4456448 | tf_op jit(solution)/shard_map/reduce_scatter | solution.py:33
  14.1 264.3 %all-gather.3.cloned.1.call-start = ((), (), s32[]{:S(2)}) async-start(), calls=%async_computation.4 | async-start | bytes 4456448 | tf_op jit(solution)/shard_map/all_gather | solution.py:34
  20.7 63.8 %collective-permute-start = (bf16[2048,1024]{0,1:T(8,128)(2,1)}, bf16[2048,1024]{0,1:T(8,128)(2,1)}, u32[]{:S(2)}, u32[]{:S(2)}) collective-permute-start(bf16[2048,1024]{0,1:T(8,128)(2,1)} %copy.12), channel_id=1, source_target_pairs={{0,1},{1,0},{2,3},{3,2},{4,5},{5,4},{6,7},{7,6},{8,9},{9,8},{10,11... | collective-permute-start | bytes 12582920 | tf_op jit(solution)/shard_map/ppermute | solution.py:12
  82.7 248.9 %all-gather.5.cloned.1.call-start = ((), (), s32[]{:S(2)}) async-start(), calls=%async_computation.6 | async-start | bytes 4456448 | tf_op jit(solution)/shard_map/all_gather | solution.py:34
  123.9 106.6 %collective-permute-start.1 = (bf16[2048,1024]{1,0:T(8,128)(2,1)}, bf16[2048,1024]{1,0:T(8,128)(2,1)}, u32[]{:S(2)}, u32[]{:S(2)}) collective-permute-start(bf16[2048,1024]{1,0:T(8,128)(2,1)} %fusion.3), channel_id=1, source_target_pairs={{0,8},{1,9},{2,10},{3,11},{4,12},{5,13},{6,14},{7,15},{8,0},{9,1},... | collective-permute-start | bytes 12582920 | tf_op jit(solution)/shard_map/ppermute | solution.py:18
  263.0 119.1 %collective-permute-start.2 = (bf16[2048,1024]{1,0:T(8,128)(2,1)}, bf16[2048,1024]{1,0:T(8,128)(2,1)}, u32[]{:S(2)}, u32[]{:S(2)}) collective-permute-start(bf16[2048,1024]{1,0:T(8,128)(2,1)} %multiply_convert_fusion.1), channel_id=1, source_target_pairs={{0,64},{16,80},{32,96},{48,112},{64,0},{80,16},{96,32},{112,48},{1... | collective-permute-start | bytes 12582920 | tf_op jit(solution)/shard_map/ppermute | solution.py:18
  331.6 50.4 %copy-start.2 = (f32[1024,1024]{1,0:T(8,128)S(1)}, f32[1024,1024]{1,0:T(8,128)}, u32[]{:S(2)}) copy-start(f32[1024,1024]{1,0:T(8,128)} %fusion.4) | copy-start | bytes 12582916
  386.2 2.0 copy-start.1
Sparse Core Ops, SparseCore 0:
  13.5 69.1 reduce-scatter.2
  85.1 143.6 reduce-scatter.4
  230.5 47.8 all-gather.2
  279.9 51.6 all-gather.4
where the time goes:
time: 426 us
  waiting for transfers between devices  263 us (62%)
  local copies, waits for them, and re-layouts  42.4 us (10%)
  other arithmetic  36.5 us (9%)
  matrix products  33.7 us (8%)
  blocking collectives  30 us (7%)
  between operations  13.9 us (3%)
  starting transfers between devices  6.44 us (2%)
    reduce_scatter x2, waiting for transfers between devices, broadcast_by_parts(): own = lax.psum_scatter(padded, axis, scatter_dimension=0, tiled=True)  165 us
    all_gather x2, waiting for transfers between devices, broadcast_by_parts(): lax.all_gather(own, axis, axis=0, tiled=True)[:len(lines)].reshape(x.shape)  53.7 us
    ppermute x2, waiting for transfers between devices, shifted(): return lax.ppermute(value, axis, pairs)  42.7 us
    all_to_all x1, blocking collectives, sum_at_owner(): parts = lax.all_to_all(split_up(x, dim, size), axis, 0, 0, tiled=True)  30 us
    gather x2, local copies, waits for them, and re-layouts, on_device(): jnp.take(whole_block, own_perm, axis=1) * own_scale[None, :]  19.8 us
    dot_general x2, matrix products, on_device(): lax.dot_general(left_half, mixed, (((0,), (0,)), ((), ())), preferred_ele...  17.8 us
    dot_general x1, matrix products, on_device(): jnp.dot(whole_block, diag_blocks, preferred_element_type=jnp.float32)  14.6 us
    gather x1, local copies, waits for them, and re-layouts, on_device(): jnp.take(mixed, perm_rows, axis=0) * scale_rows[:, None]  13.7 us
  transfers between devices with their start and end apart: 7, of which 5 were waited for; matrix products, arithmetic and copies ran while one was open for 23% of the time, Pallas kernels for 0%

commit v1 on v0

--- a/solution.py
+++ b/solution.py
@@ -31,7 +31,9 @@
     )
     padded = rows_for(lines, lax.axis_size(axis))
     own = lax.psum_scatter(padded, axis, scatter_dimension=0, tiled=True)
-    return lax.all_gather(own, axis, axis=0, tiled=True)[: len(lines)].reshape(x.shape)
+    return jnp.concatenate(
+        lax.all_to_all(jnp.stack([own] * lax.axis_size(axis)), axis, 0, 0), axis=0
+    )[: len(lines)].reshape(x.shape)
 
 
 def split_up(x, dim, size):

time: 426 us -> 482 us (1.13)
  waiting for transfers between devices: 263 us -> 293 us
  starting transfers between devices: 6.44 us -> 22.7 us
  local copies, waits for them, and re-layouts: 42.4 us -> 49.4 us
    all_gather x2 -> x0, waiting for transfers between devices: 53.7 us -> none  [broadcast_by_parts(): lax.all_gather(own, axis, axis=0, tiled=True)[:len(lines)].reshape(x.shape)]
    ppermute x2, waiting for transfers between devices: 42.7 us -> 82.4 us  [shifted(): return lax.ppermute(value, axis, pairs)]
    reduce_scatter x2, waiting for transfers between devices: 165 us -> 199 us  [broadcast_by_parts(): own = lax.psum_scatter(padded, axis, scatter_dimension=0, tiled=True)]
    all_to_all x0 -> x2, starting transfers between devices: none -> 13.7 us  [broadcast_by_parts(): lax.all_to_all(jnp.stack([own] * lax.axis_size(axis)), axis, 0, 0)]
    another operation x0 -> x2, local copies, waits for them, and re-layouts: none -> 6.99 us  [broadcast_by_parts(): jnp.stack([own] * lax.axis_size(axis))]
    all_to_all x0 -> x2, waiting for transfers between devices: none -> 6.15 us  [broadcast_by_parts(): lax.all_to_all(jnp.stack([own] * lax.axis_size(axis)), axis, 0, 0)]
    ppermute x1, waiting for transfers between devices: 0.01 us -> 5.36 us  [partner_2(): return lax.ppermute(value, axis, pairs)]
  transfers between devices with their start and end apart: 7 -> 7, of which waited for: 5 -> 5; matrix products, arithmetic and copies ran while one was open for 23% -> 22% of each run, Pallas kernels for 0% -> 0%
where the time goes in v1:
time: 482 us; the launch traced here: 481 us
  waiting for transfers between devices  293 us (61%)
  local copies, waits for them, and re-layouts  49.4 us (10%)
  other arithmetic  36.7 us (8%)
  matrix products  33.7 us (7%)
  blocking collectives  31.5 us (7%)
  starting transfers between devices  22.7 us (5%)
  between operations  14.2 us (3%)
    reduce_scatter x2, waiting for transfers between devices, broadcast_by_parts(): own = lax.psum_scatter(padded, axis, scatter_dimension=0, tiled=True)  199 us
    ppermute x2, waiting for transfers between devices, shifted(): return lax.ppermute(value, axis, pairs)  82.4 us
    all_to_all x1, blocking collectives, sum_at_owner(): parts = lax.all_to_all(split_up(x, dim, size), axis, 0, 0, tiled=True)  31.5 us
    gather x2, local copies, waits for them, and re-layouts, on_device(): jnp.take(whole_block, own_perm, axis=1) * own_scale[None, :]  19.8 us
    dot_general x2, matrix products, on_device(): lax.dot_general(left_half, mixed, (((0,), (0,)), ((), ())), preferred_ele...  17.8 us
    dot_general x1, matrix products, on_device(): jnp.dot(whole_block, diag_blocks, preferred_element_type=jnp.float32)  14.6 us
    all_to_all x2, starting transfers between devices, broadcast_by_parts(): lax.all_to_all(jnp.stack([own] * lax.axis_size(axis)), axis, 0, 0)  13.7 us
    gather x1, local copies, waits for them, and re-layouts, on_device(): jnp.take(mixed, perm_rows, axis=0) * scale_rows[:, None]  13.7 us
  transfers between devices with their start and end apart: 7, of which 5 were waited for; matrix products, arithmetic and copies ran while one was open for 22% of the time, Pallas kernels for 0%

profile of v1, /device:TPU:1, one launch (start us, length us, event | category | flops | bytes accessed | tf_op | source)
XLA Modules:
  0.0 481.4 jit_solution(15025699185365642854)
XLA Ops:
  7.2 6.1 %broadcast_select_fusion.3 = (bf16[2048,1024]{1,0:T(8,128)(2,1)}, bf16[2048,1024]{1,0:T(8,128)(2,1)}) fusion(bf16[2048,1024]{1,0:T(8,128)(2,1)} %param.6, pred[]{:T(512)S(6)} %eq.16, pred[]{:T(512)S(6)} %eq.18), kind=kLoop, calls=%fused_computation.14 | loop fusion | flops 4194304 | bytes 12582914 | tf_op jit(solution)/shard_map/jit(_where)/select_n | solution.py:29
  13.4 6.5 %copy.12 = bf16[2048,1024]{0,1:T(8,128)(2,1)} copy(bf16[2048,1024]{1,0:T(8,128)(2,1)} %param.5) | data formatting | bytes 8388608 | tf_op args[0]
  20.0 1.4 collective-permute-start
  21.4 0.8 dynamic_slice.23
  22.3 0.8 compare_select_fusion.1
  23.1 5.4 %collective-permute-done = bf16[2048,1024]{0,1:T(8,128)(2,1)} collective-permute-done((bf16[2048,1024]{0,1:T(8,128)(2,1)}, bf16[2048,1024]{0,1:T(8,128)(2,1)}, u32[]{:S(2)}, u32[]{:S(2)}) %collective-permute-start) | collective-permute-done | bytes 4194336 | tf_op jit(solution)/shard_map/ppermute | solution.py:12
  28.5 5.9 %broadcast_select_fusion.2 = (bf16[2048,1024]{0,1:T(8,128)(2,1)}, bf16[2048,1024]{0,1:T(8,128)(2,1)}) fusion(bf16[2048,1024]{0,1:T(8,128)(2,1)} %copy.12, bf16[2048,1024]{0,1:T(8,128)(2,1)} %collective-permute-done, pred[]{:T(512)S(6)} %eq.17), kind=kLoop, calls=%fused_computation.13 | loop fusion | flops 4194304 | bytes 16777216 | tf_op jit(solution)/shard_map/jit(_where)/select_n | solution.py:62
  34.4 8.5 %pad_maximum_fusion = bf16[2048,2048]{0,1:T(8,128)(2,1)} fusion(bf16[2048,1024]{0,1:T(8,128)(2,1)} %get-tuple-element.7, bf16[2048,1024]{0,1:T(8,128)(2,1)} %get-tuple-element.6), kind=kLoop, calls=%fused_computation.2 | loop fusion | flops 16777216 | bytes 16777216 | tf_op jit(solution)/shard_map/concatenate | solution.py:64
  42.9 13.4 %gather_fusion = bf16[1024,2048]{1,0:T(8,128)(2,1)} fusion(bf16[2048,2048]{0,1:T(8,128)(2,1)} %pad_maximum_fusion, s32[1024]{0:T(1024)S(1)} %broadcast_clamp_fusion.1), kind=kCustom, calls=%fused_computation | custom fusion | bytes 8392704 | tf_op jit(solution)/shard_map/jit(_take)/gather | solution.py:69
  56.3 6.4 %copy.14 = bf16[1024,2048]{0,1:T(8,128)(2,1)} copy(bf16[1024,2048]{1,0:T(8,128)(2,1)} %gather_fusion) | data formatting | bytes 8388608 | tf_op jit(solution)/shard_map/jit(_take)/gather | solution.py:69
  62.7 5.4 %fusion.3 = bf16[2048,1024]{1,0:T(8,128)(2,1)} fusion(f32[1024]{0:T(1024)S(1)} %bitcast.26, bf16[1024,2048]{0,1:T(8,128)(2,1)} %copy.14, pred[1024]{0:T(1024)(128)(4,1)S(1)} %compare_and_fusion.1), kind=kLoop, calls=%fused_computation.10 | loop fusion | flops 8388608 | bytes 8393728 | tf_op jit(solution)/shard_map/convert_element_type | solution.py:69
  68.1 2.8 collective-permute-start.1
  70.9 98.3 %reduce-scatter.3.cloned.1.call-done = bf16[128,1024]{1,0:T(8,128)(2,1)} async-done(((bf16[2048,1024]{1,0:T(8,128)(2,1)}), bf16[128,1024]{1,0:T(8,128)(2,1)}) %reduce-scatter.3.cloned.1.call-update) | async-done | bytes 262160 | tf_op jit(solution)/shard_map/reduce_scatter | solution.py:33
  169.2 3.5 stack.4
  172.7 6.6 %all-to-all-start = ((bf16[16,128,1024]{2,1,0:T(8,128)(2,1)}), bf16[16,128,1024]{2,1,0:T(8,128)(2,1)}, u32[]{:S(2)}, u32[]{:S(2)}) async-start(bf16[16,128,1024]{2,1,0:T(8,128)(2,1)} %stack.4), calls=%async_computation.1 | async-start | bytes 8388608 | tf_op jit(solution)/shard_map/all_to_all | solution.py:35
  179.3 0.8 constant_dynamic-slice_fusion
  180.1 0.9 compare_select_fusion
  181.0 101.1 %reduce-scatter.5.cloned.1.call-done = bf16[128,1024]{1,0:T(8,128)(2,1)} async-done(((bf16[2048,1024]{1,0:T(8,128)(2,1)}), bf16[128,1024]{1,0:T(8,128)(2,1)}) %reduce-scatter.5.cloned.1.call-update) | async-done | bytes 262160 | tf_op jit(solution)/shard_map/reduce_scatter | solution.py:33
  282.1 3.5 stack.5
  285.6 7.1 %all-to-all-start.1 = ((bf16[16,128,1024]{2,1,0:T(8,128)(2,1)}), bf16[16,128,1024]{2,1,0:T(8,128)(2,1)}, u32[]{:S(2)}, u32[]{:S(2)}) async-start(bf16[16,128,1024]{2,1,0:T(8,128)(2,1)} %stack.5), calls=%async_computation.3 | async-start | bytes 8388608 | tf_op jit(solution)/shard_map/all_to_all | solution.py:35
  292.7 14.6 %add_convert_fusion = bf16[2048,1024]{1,0:T(8,128)(2,1)} fusion(bf16[2048,1024]{1,0:T(8,128)(2,1)} %collective-permute-done.1, bf16[2048,1024]{1,0:T(8,128)(2,1)} %param.6, bf16[2048,1024]{0,1:T(8,128)(2,1)} %get-tuple-element.7, bf16[2048,1024]{0,1:T(8,128)(2,1)} %get-tuple-element.6), kind=kOutput, calls=%fused_computation.9 | convolution fusion | flops 8613003264 | bytes 20971520 | tf_op jit(solution)/shard_map/dot_general | solution.py:72
  307.3 13.7 %gather_fusion.1 = bf16[2048,1024]{1,0:T(8,128)(2,1)} fusion(bf16[2048,1024]{1,0:T(8,128)(2,1)} %add_convert_fusion, s32[2048]{0:T(1024)S(1)} %broadcast_clamp_fusion), kind=kCustom, calls=%fused_computation.1 | custom fusion | bytes 8396800 | tf_op jit(solution)/shard_map/jit(_take)/gather | solution.py:78
  321.0 4.1 multiply_convert_fusion.1
  325.1 4.7 collective-permute-start.2
  329.8 10.1 %fusion.4 = f32[1024,1024]{1,0:T(8,128)} fusion(bf16[2048,1024]{1,0:T(8,128)(2,1)} %bitcast, bf16[2048,1024]{1,0:T(8,128)(2,1)} %add_convert_fusion), kind=kOutput, calls=%fused_computation.27 | convolution fusion | flops 4294967296 | bytes 12582912 | tf_op jit(solution)/shard_map/dot_general | solution.py:86
  339.9 6.1 %all-to-all-done.1 = bf16[16,128,1024]{2,1,0:T(8,128)(2,1)} async-done(((bf16[16,128,1024]{2,1,0:T(8,128)(2,1)}), bf16[16,128,1024]{2,1,0:T(8,128)(2,1)}, u32[]{:S(2)}, u32[]{:S(2)}) %all-to-all-start.1) | async-done | bytes 4194336 | tf_op jit(solution)/shard_map/all_to_all | solution.py:35
  346.1 7.7 %fusion.5 = f32[1024,1024]{1,0:T(8,128)S(1)} fusion(bf16[2048,1024]{1,0:T(8,128)(2,1)} %bitcast.6, bf16[2048,1024]{1,0:T(8,128)(2,1)} %add_convert_fusion), kind=kOutput, calls=%fused_computation.28 | convolution fusion | flops 4294967296 | bytes 12582912 | tf_op jit(solution)/shard_map/dot_general | solution.py:86
  353.8 82.4 %collective-permute-done.2 = bf16[2048,1024]{1,0:T(8,128)(2,1)} collective-permute-done((bf16[2048,1024]{1,0:T(8,128)(2,1)}, bf16[2048,1024]{1,0:T(8,128)(2,1)}, u32[]{:S(2)}, u32[]{:S(2)}) %collective-permute-start.2) | collective-permute-done | bytes 4194336 | tf_op jit(solution)/shard_map/ppermute | solution.py:18
  436.2 4.1 fusion.2
  440.3 1.3 fusion.6
  442.3 31.5 %all_to_all.15 = f32[16,128,256]{2,1,0:T(8,128)S(1)} all-to-all(f32[16,128,256]{2,1,0:T(8,128)S(1)} %bitcast.22), channel_id=1, replica_groups=mesh['row'=8,'col'=16] {'col'}, dimensions={0} | all-to-all | bytes 4194304 | tf_op jit(solution)/shard_map/all_to_all | solution.py:47
  473.8 0.8 reduce_sum.9
  (18 shorter events, 0.9 us)
Async XLA Ops:
  7.2 433.1 %copy-start = (bf16[1024,256]{1,0:T(8,128)(2,1)S(1)}, bf16[1024,256]{1,0:T(8,128)(2,1)}, u32[]{:S(2)}) copy-start(bf16[1024,256]{1,0:T(8,128)(2,1)} %param.9) | copy-start | bytes 1572868
  7.2 162.0 %reduce-scatter.3.cloned.1.call-start = ((), (), s32[]{:S(2)}) async-start(), calls=%async_computation.5 | async-start | bytes 4456448 | tf_op jit(solution)/shard_map/reduce_scatter | solution.py:33
  13.4 268.7 %reduce-scatter.5.cloned.1.call-start = ((), (), s32[]{:S(2)}) async-start(), calls=%async_computation.6 | async-start | bytes 4456448 | tf_op jit(solution)/shard_map/reduce_scatter | solution.py:33
  20.0 8.6 %collective-permute-start = (bf16[2048,1024]{0,1:T(8,128)(2,1)}, bf16[2048,1024]{0,1:T(8,128)(2,1)}, u32[]{:S(2)}, u32[]{:S(2)}) collective-permute-start(bf16[2048,1024]{0,1:T(8,128)(2,1)} %copy.12), channel_id=1, source_target_pairs={{0,1},{1,0},{2,3},{3,2},{4,5},{5,4},{6,7},{7,6},{8,9},{9,8},{10,11... | collective-permute-start | bytes 12582920 | tf_op jit(solution)/shard_map/ppermute | solution.py:12
  68.1 224.6 %collective-permute-start.1 = (bf16[2048,1024]{1,0:T(8,128)(2,1)}, bf16[2048,1024]{1,0:T(8,128)(2,1)}, u32[]{:S(2)}, u32[]{:S(2)}) collective-permute-start(bf16[2048,1024]{1,0:T(8,128)(2,1)} %fusion.3), channel_id=1, source_target_pairs={{0,8},{1,9},{2,10},{3,11},{4,12},{5,13},{6,14},{7,15},{8,0},{9,1},... | collective-permute-start | bytes 12582920 | tf_op jit(solution)/shard_map/ppermute | solution.py:18
  172.7 109.4 %all-to-all-start = ((bf16[16,128,1024]{2,1,0:T(8,128)(2,1)}), bf16[16,128,1024]{2,1,0:T(8,128)(2,1)}, u32[]{:S(2)}, u32[]{:S(2)}) async-start(bf16[16,128,1024]{2,1,0:T(8,128)(2,1)} %stack.4), calls=%async_computation.1 | async-start | bytes 8388608 | tf_op jit(solution)/shard_map/all_to_all | solution.py:35
  285.6 60.5 %all-to-all-start.1 = ((bf16[16,128,1024]{2,1,0:T(8,128)(2,1)}), bf16[16,128,1024]{2,1,0:T(8,128)(2,1)}, u32[]{:S(2)}, u32[]{:S(2)}) async-start(bf16[16,128,1024]{2,1,0:T(8,128)(2,1)} %stack.5), calls=%async_computation.3 | async-start | bytes 8388608 | tf_op jit(solution)/shard_map/all_to_all | solution.py:35
  325.1 111.0 %collective-permute-start.2 = (bf16[2048,1024]{1,0:T(8,128)(2,1)}, bf16[2048,1024]{1,0:T(8,128)(2,1)}, u32[]{:S(2)}, u32[]{:S(2)}) collective-permute-start(bf16[2048,1024]{1,0:T(8,128)(2,1)} %multiply_convert_fusion.1), channel_id=1, source_target_pairs={{0,64},{16,80},{32,96},{48,112},{64,0},{80,16},{96,32},{112,48},{1... | collective-permute-start | bytes 12582920 | tf_op jit(solution)/shard_map/ppermute | solution.py:18
  346.1 90.1 %copy-start.1 = (f32[1024,1024]{1,0:T(8,128)S(1)}, f32[1024,1024]{1,0:T(8,128)}, u32[]{:S(2)}) copy-start(f32[1024,1024]{1,0:T(8,128)} %fusion.4) | copy-start | bytes 12582916
  440.3 2.0 copy-start.2
Sparse Core Ops, SparseCore 0:
  13.5 155.6 reduce-scatter.2
  171.6 110.4 reduce-scatter.4
